TPU v7x, 256 devices: a whole 4x4x8 slice. The times are simulated.
256 devices in a mesh: row: 8 (over z), col: 32 (over y, x, core).
Axes of the slice: x: 4, y: 4, z: 8, core: 2. Of those that a mesh axis runs over, the one named last changes fastest.
Arguments:
- ancestor_inverse: bfloat16 [24576, 24576], P('row', 'col'), may hold values from -6 to 6
- factor_slots: bfloat16 [3, 16384, 512], P(None, ('row', 'col')), may hold values from -0.25 to 0.25
- slot_tiles: int32 [3, 64], replicated, may hold values from -1 to 95, as said below
- parent_factor: bfloat16 [2, 512, 512], replicated, may hold values from -0.25 to 0.25
- diag_inverse: float32 [3, 512, 512], replicated, may hold values from -6 to 6
Outputs:
- inverse_panels: bfloat16 [3, 24576, 512], P(None, ('row', 'col'))
- diag_blocks: float32 [3, 512, 512], replicated
- parent_blocks: float32 [2, 512, 512], replicated
Inputs may be any that keep to these rules, and one draw needn't show every extreme that they name: `slot_tiles`: entries b * 2 to b * 2 + 1 of a supernode's row are the slots of column block b: each is -1 (empty) or names a tile from b * 3 to b * 3 + 2, no tile twice; in each supernode some block has all its slots filled. `factor_slots`: rows of an empty slot are not part of the factor.
All inputs are finite; a program needn't handle non-finite values.
Results may differ from a plain program's by a relative error of at most 0.00075.
Values may be sent and summed in bfloat16 or wider, within the bound.
No kernel may reach another device: no remote copies, remote signals or barrier semaphores. Data moves between devices by JAX's collectives and lax.ppermute only.
A program may use at most 128 MiB of HBM per device.

v0:
```python
import jax
import jax.numpy as jnp
from jax import lax
from jax.sharding import PartitionSpec as P

TILE = 256
CAP = 2
exact_mode = lax.Precision.HIGHEST


def spread(shard, axis, root):
    mine = lax.axis_index(axis) == root
    return lax.psum(jnp.where(mine, shard, jnp.zeros_like(shard)), axis)


def padded_block(slot_data, slot_ids, block_index, tiles_per_block, tile_rows):
    local_tile = slot_ids - block_index * tiles_per_block
    pieces = []
    for tile_index in range(tiles_per_block):
        chosen = jnp.zeros((tile_rows, slot_data.shape[1]), slot_data.dtype)
        for member in range(slot_ids.shape[0]):
            chosen = jnp.where(
                local_tile[member] == tile_index,
                slot_data[member * tile_rows : (member + 1) * tile_rows],
                chosen,
            )
        pieces.append(chosen)
    return jnp.concatenate(pieces, axis=0)


def chosen_columns(inverse_block, slot_ids, block_index, tiles_per_block, tile_rows):
    local_tile = jnp.clip(slot_ids - block_index * tiles_per_block, 0, tiles_per_block - 1)
    pieces = [
        lax.dynamic_slice_in_dim(inverse_block, local_tile[member] * tile_rows, tile_rows, 1)
        for member in range(slot_ids.shape[0])
    ]
    return jnp.concatenate(pieces, axis=1)


def masked_rows(slot_data, slot_ids, tile_rows):
    live_rows = jnp.repeat(slot_ids >= 0, tile_rows)
    return jnp.where(live_rows[:, None], slot_data, jnp.zeros_like(slot_data))


def on_device(ancestor_inverse, factor_slots, slot_tiles, parent_factor, diag_inverse):
    row_count = lax.axis_size("row")
    col_count = lax.axis_size("col")
    row_index = lax.axis_index("row")
    col_index = lax.axis_index("col")
    block_rows, block_cols = ancestor_inverse.shape
    tile_rows = TILE
    tiles_per_block = block_cols // tile_rows
    node_count = factor_slots.shape[0]
    slot_count = CAP
    slot_rows = slot_count * tile_rows
    groups_per_row = col_count // row_count
    panel_rows = block_rows // col_count
    own_block = row_index * groups_per_row + col_index // row_count
    own_offset = col_index % row_count * panel_rows
    slot_start = col_index % groups_per_row * slot_rows
    owner_row = col_index // groups_per_row

    def finish(node, first_total, second_total, prev_diag):
        if node == 0:
            return (diag_inverse[0] - first_total, None)
        parent_link = parent_factor[node - 1].astype(jnp.float32)
        upper = -(second_total + jnp.dot(prev_diag, parent_link, precision=exact_mode))
        diagonal = (
            diag_inverse[node] - first_total - jnp.dot(parent_link.T, upper, precision=exact_mode)
        )
        return (diagonal, upper)

    def node_sums(node, first_part, second_part):
        if node == 0:
            return (lax.psum(first_part, ("row", "col")), None)
        return lax.psum((first_part, second_part), ("row", "col"))

    panels = []
    diagonals = []
    parents = []
    previous = None
    prev_diag = None
    for node in range(node_count):
        row_slots = lax.all_gather(factor_slots[node], "col", axis=0, tiled=True)
        mine = lax.dynamic_slice_in_dim(row_slots, slot_start, slot_rows, 0)
        col_slots = spread(mine, "row", owner_row)
        tiles_node = slot_tiles[node]
        col_ids = lax.dynamic_slice_in_dim(tiles_node, col_index * slot_count, slot_count)
        prepare_columns = chosen_columns(
            ancestor_inverse, col_ids, col_index, tiles_per_block, tile_rows
        )
        prepare_weights = masked_rows(col_slots, col_ids, tile_rows)
        own_ids = lax.dynamic_slice_in_dim(tiles_node, own_block * slot_count, slot_count)
        own_slots = lax.dynamic_slice_in_dim(
            row_slots, col_index // row_count * slot_rows, slot_rows, 0
        )
        own_padded = padded_block(own_slots, own_ids, own_block, tiles_per_block, tile_rows)
        own_rows = lax.dynamic_slice_in_dim(own_padded, own_offset, panel_rows, 0)
        row_padded = None
        columns, weights, own_rows, row_padded = (
            prepare_columns,
            prepare_weights,
            own_rows.astype(jnp.float32),
            row_padded,
        )
        second_part = None
        if node > 0:
            second_part = jnp.dot(previous.T, own_rows, precision=exact_mode)
        summed = lax.psum_scatter(
            jnp.dot(columns, weights, preferred_element_type=jnp.float32),
            "col",
            scatter_dimension=0,
            tiled=True,
        )
        column = -summed
        if node > 0:
            advance_parent_link = parent_factor[node - 1].astype(jnp.float32)
            column = column - jnp.dot(previous, advance_parent_link, precision=exact_mode)
        first_part = jnp.dot(own_rows.T, column, precision=exact_mode)
        first_total, second_total = node_sums(node, first_part, second_part)
        diagonal, upper = finish(node, first_total, second_total, prev_diag)
        panels.append(column.astype(jnp.bfloat16))
        diagonals.append(diagonal)
        if node > 0:
            parents.append(upper)
        previous = column
        prev_diag = diagonal
    return (jnp.stack(panels), jnp.stack(diagonals), jnp.stack(parents))


def solution(mesh):
    placed = (P("row", "col"), P(None, ("row", "col"), None), P(), P(), P())
    return jax.shard_map(
        on_device,
        mesh=mesh,
        in_specs=placed,
        out_specs=(P(None, ("row", "col"), None), P(), P()),
        check_vma=False,
    )
```

profile of v0, /device:TPU:8, one launch (start us, length us, event | category | flops | bytes accessed | tf_op | source)
XLA Modules:
  0.0 841.9 jit_solution(13287973406344088835)
XLA Ops:
  10.4 51.9 %all-gather.9.cloned.1.call-done = bf16[1,2048,512]{2,1,0:T(8,128)(2,1)} async-done(((bf16[1,64,512]{2,1,0:T(8,128)(2,1)}), bf16[1,2048,512]{2,1,0:T(8,128)(2,1)}) %all-gather.9.cloned.1.call-update) | async-done | bytes 2097168 | tf_op jit(solution)/shard_map/all_gather | solution.py:84
  62.3 1.9 select_bitcast_fusion.1
  64.2 49.2 %all-gather.7.cloned.1.call-done = bf16[1,2048,512]{2,1,0:T(8,128)(2,1)} async-done(((bf16[1,64,512]{2,1,0:T(8,128)(2,1)}), bf16[1,2048,512]{2,1,0:T(8,128)(2,1)}) %all-gather.7.cloned.1.call-update) | async-done | bytes 2097168 | tf_op jit(solution)/shard_map/all_gather | solution.py:84
  113.4 1.9 select_bitcast_fusion.2
  115.3 49.2 %all-gather.11.cloned.1.call-done = bf16[1,2048,512]{2,1,0:T(8,128)(2,1)} async-done(((bf16[1,64,512]{2,1,0:T(8,128)(2,1)}), bf16[1,2048,512]{2,1,0:T(8,128)(2,1)}) %all-gather.11.cloned.1.call-update) | async-done | bytes 2097168 | tf_op jit(solution)/shard_map/all_gather | solution.py:84
  164.5 1.9 select_bitcast_fusion
  172.6 6.8 constant_dynamic-slice_fusion.4
  179.5 66.0 %all-reduce.7.cloned.1.call-done = (bf16[512,512]{1,0:T(8,128)(2,1)}, bf16[512,512]{1,0:T(8,128)(2,1)}, bf16[512,512]{1,0:T(8,128)(2,1)}) async-done(((bf16[512,512]{1,0:T(8,128)(2,1)}, bf16[512,512]{1,0:T(8,128)(2,1)}, bf16[512,512]{1,0:T(8,128)(2,1)}), (bf16[512,512]{1,0:T(8,128)(2,1)}, bf16[512,512]{1,0:T(8,128)(2,1)}, bf16[512,512]{1,0:T(8,128)(2,1)})) %all-reduce.7.cloned.1.call-update) | async-done | bytes 1572880 | tf_op jit(solution)/shard_map/psum | solution.py:13
  245.4 6.5 fusion.4
  252.2 6.5 fusion
  258.8 5.5 fusion.8
  278.5 2.0 select_bitcast_fusion.10
  281.7 63.3 %reduce-scatter.6.cloned.1.call-done = f32[96,512]{1,0:T(8,128)} async-done(((f32[3072,512]{1,0:T(8,128)}), f32[96,512]{1,0:T(8,128)}) %reduce-scatter.6.cloned.1.call-update) | async-done | bytes 196624 | tf_op jit(solution)/shard_map/reduce_scatter | solution.py:109
  345.0 97.1 %reduce-scatter.4.cloned.1.call-done = f32[96,512]{1,0:T(8,128)} async-done(((f32[3072,512]{1,0:T(8,128)}), f32[96,512]{1,0:T(8,128)}) %reduce-scatter.4.cloned.1.call-update) | async-done | bytes 196624 | tf_op jit(solution)/shard_map/reduce_scatter | solution.py:109
  443.5 1.7 fusion.69
  445.2 94.2 %reduce-scatter.8.cloned.1.call-done = f32[96,512]{1,0:T(8,128)} async-done(((f32[3072,512]{1,0:T(8,128)}), f32[96,512]{1,0:T(8,128)}) %reduce-scatter.8.cloned.1.call-update) | async-done | bytes 196624 | tf_op jit(solution)/shard_map/reduce_scatter | solution.py:109
  540.7 1.7 fusion.67
  542.5 1.7 fusion.64
  544.2 1.7 fusion.39
  545.8 1.8 fusion.41
  548.5 274.5 %all-reduce.5.cloned.1.call-done = (f32[512,512]{1,0:T(8,128)}, f32[512,512]{1,0:T(8,128)}, f32[512,512]{1,0:T(8,128)}, f32[512,512]{1,0:T(8,128)}, f32[512,512]{1,0:T(8,128)}) async-done(((f32[512,512]{1,0:T(8,128)}, f32[512,512]{1,0:T(8,128)}, f32[512,512]{1,0:T(8,128)}, f32[512,512]{1,0:T(8,128)}, f32[512,512]{1,0:T(8,128)}), (f32[512,512]{1,0:T(8,128)}, f32[512,512]{1,0:T(8,128)}, f32[512,512]{1,0:T(8,128)}, ...) | async-done | bytes 5242896 | tf_op jit(solution)/shard_map/psum | solution.py:76
  823.1 1.9 fusion.29
  825.6 2.6 fusion.13
  833.0 2.0 pad_maximum_fusion
  (63 shorter events, 18.7 us)
Async XLA Ops:
  7.2 159.4 %copy-start.8 = (s32[3,64]{1,0:T(4,128)S(1)}, s32[3,64]{1,0:T(4,128)}, u32[]{:S(2)}) copy-start(s32[3,64]{1,0:T(4,128)} %param.7) | copy-start | bytes 2308
  7.2 55.1 %all-gather.9.cloned.1.call-start = ((), (), s32[]{:S(2)}) async-start(), calls=%async_computation.7 | async-start | bytes 2162688 | tf_op jit(solution)/shard_map/all_gather | solution.py:84
  8.8 104.6 %all-gather.7.cloned.1.call-start = ((), (), s32[]{:S(2)}) async-start(), calls=%async_computation.6 | async-start | bytes 2162688 | tf_op jit(solution)/shard_map/all_gather | solution.py:84
  9.6 154.9 %all-gather.11.cloned.1.call-start = ((), (), s32[]{:S(2)}) async-start(), calls=%async_computation.8 | async-start | bytes 2162688 | tf_op jit(solution)/shard_map/all_gather | solution.py:84
  10.3 235.1 %all-reduce.7.cloned.1.call-start = ((), (), s32[]{:S(2)}) async-start(), calls=%async_computation.10 | async-start | bytes 3145728 | tf_op jit(solution)/shard_map/psum | solution.py:13
  166.5 178.5 %reduce-scatter.6.cloned.1.call-start = ((), (), s32[]{:S(2)}) async-start(), calls=%async_computation.4 | async-start | bytes 6488064 | tf_op jit(solution)/shard_map/reduce_scatter | solution.py:109
  252.0 190.1 %reduce-scatter.4.cloned.1.call-start = ((), (), s32[]{:S(2)}) async-start(), calls=%async_computation.3 | async-start | bytes 6488064 | tf_op jit(solution)/shard_map/reduce_scatter | solution.py:109
  258.7 280.7 %reduce-scatter.8.cloned.1.call-start = ((), (), s32[]{:S(2)}) async-start(), calls=%async_computation.5 | async-start | bytes 6488064 | tf_op jit(solution)/shard_map/reduce_scatter | solution.py:109
  264.4 177.7 %copy-start = (bf16[2,512,512]{2,1,0:T(8,128)(2,1)S(1)}, bf16[2,512,512]{2,1,0:T(8,128)(2,1)}, u32[]{:S(2)}) copy-start(bf16[2,512,512]{2,1,0:T(8,128)(2,1)} %param.8) | copy-start | bytes 3145732
  264.4 558.7 %all-reduce.5.cloned.1.call-start = ((), (), s32[]{:S(2)}) async-start(), calls=%async_computation.9 | async-start | bytes 10485760 | tf_op jit(solution)/shard_map/psum | solution.py:76
  443.5 100.7 %copy-start.2 = (f32[96,512]{1,0:T(8,128)S(1)}, f32[96,512]{1,0:T(8,128)}, u32[]{:S(2)}) copy-start(f32[96,512]{1,0:T(8,128)} %reduce-scatter.4.cloned.1.call-done) | copy-start | bytes 589828
  540.7 5.1 copy-start.4
  540.7 5.1 copy-start.5
  823.0 2.5 copy-start.1
  825.0 3.2 copy-start.7
  828.2 1.2 copy-start.3
  828.2 2.2 copy-start.6
Sparse Core Ops, SparseCore 0:
  11.1 51.0 all-gather.8
  65.4 47.9 all-gather.6
  116.5 47.9 all-gather.10
  167.0 78.4 all-reduce.6
  252.1 92.8 reduce-scatter.5
  348.9 93.1 reduce-scatter.3
  446.1 93.2 reduce-scatter.7
  547.8 275.1 all-reduce.4
where the time goes:
time: 843 us; the launch traced here: 842 us
  waiting for transfers between devices  747 us (89%)
  matrix products  35.6 us (4%)
  between operations  29.7 us (4%)
  other arithmetic  16.8 us (2%)
  local copies, waits for them, and re-layouts  12.5 us (1%)
    psum x1, waiting for transfers between devices, node_sums(): return lax.psum((first_part, second_part), ('row', 'col'))  275 us
    reduce_scatter x3, waiting for transfers between devices, on_device(): lax.psum_scatter(jnp.dot(columns, weights, preferred_element_type=jnp.flo...  255 us
    all_gather x3, waiting for transfers between devices, on_device(): row_slots = lax.all_gather(factor_slots[node], 'col', axis=0, tiled=True)  150 us
    psum x1, waiting for transfers between devices, spread(): return lax.psum(jnp.where(mine, shard, jnp.zeros_like(shard)), axis)  66 us
    dot_general x3, matrix products, on_device(): jnp.dot(columns, weights, preferred_element_type=jnp.float32)  18.5 us
  transfers between devices with their start and end apart: 8, of which 8 were waited for; matrix products, arithmetic and copies ran while one was open for 4% of the time, Pallas kernels for 0%

commit v1 on v0

--- a/solution.py
+++ b/solution.py
@@ -6,6 +6,12 @@
 TILE = 256
 CAP = 2
 exact_mode = lax.Precision.HIGHEST
+
+
+def _try_all_entries(raw):
+    for q in ("col", "row"):
+        raw = lax.psum(raw, q)
+    return raw
 
 
 def spread(shard, axis, root):
@@ -73,7 +79,7 @@
     def node_sums(node, first_part, second_part):
         if node == 0:
             return (lax.psum(first_part, ("row", "col")), None)
-        return lax.psum((first_part, second_part), ("row", "col"))
+        return _try_all_entries((first_part, second_part))
 
     panels = []
     diagonals = []

time: 843 us -> 1060 us (1.26)
  waiting for transfers between devices: 747 us -> 965 us
    psum x1 -> x3, waiting for transfers between devices: 275 us -> 486 us  [the longest x1 264 us: node_sums(): return (lax.psum(first_part, ('row', 'col')), None)]
  transfers between devices with their start and end apart: 8 -> 10, of which waited for: 8 -> 10; matrix products, arithmetic and copies ran while one was open for 4% -> 4% of each run, Pallas kernels for 0% -> 0%
where the time goes in v1:
time: 1060 us
  waiting for transfers between devices  965 us (91%)
  matrix products  35.8 us (3%)
  between operations  29.5 us (3%)
  other arithmetic  15.8 us (1%)
  local copies, waits for them, and re-layouts  11.8 us (1%)
    psum x1, waiting for transfers between devices, node_sums(): return (lax.psum(first_part, ('row', 'col')), None)  264 us
    reduce_scatter x3, waiting for transfers between devices, on_device(): lax.psum_scatter(jnp.dot(columns, weights, preferred_element_type=jnp.flo...  261 us
    psum x2, waiting for transfers between devices, _try_all_entries(): raw = lax.psum(raw, q)  222 us
    all_gather x3, waiting for transfers between devices, on_device(): row_slots = lax.all_gather(factor_slots[node], 'col', axis=0, tiled=True)  150 us
    psum x1, waiting for transfers between devices, spread(): return lax.psum(jnp.where(mine, shard, jnp.zeros_like(shard)), axis)  66 us
  transfers between devices with their start and end apart: 10, of which 10 were waited for; matrix products, arithmetic and copies ran while one was open for 4% of the time, Pallas kernels for 0%

profile of v1, /device:TPU:8, one launch (start us, length us, event | category | flops | bytes accessed | tf_op | source)
XLA Modules:
  0.0 1058.6 jit_solution(10996331505995891116)
XLA Ops:
  10.4 51.9 %all-gather.9.cloned.1.call-done = bf16[1,2048,512]{2,1,0:T(8,128)(2,1)} async-done(((bf16[1,64,512]{2,1,0:T(8,128)(2,1)}), bf16[1,2048,512]{2,1,0:T(8,128)(2,1)}) %all-gather.9.cloned.1.call-update) | async-done | bytes 2097168 | tf_op jit(solution)/shard_map/all_gather | solution.py:90
  62.3 1.9 select_bitcast_fusion.1
  64.2 49.2 %all-gather.7.cloned.1.call-done = bf16[1,2048,512]{2,1,0:T(8,128)(2,1)} async-done(((bf16[1,64,512]{2,1,0:T(8,128)(2,1)}), bf16[1,2048,512]{2,1,0:T(8,128)(2,1)}) %all-gather.7.cloned.1.call-update) | async-done | bytes 2097168 | tf_op jit(solution)/shard_map/all_gather | solution.py:90
  113.4 1.9 select_bitcast_fusion.2
  115.3 49.2 %all-gather.11.cloned.1.call-done = bf16[1,2048,512]{2,1,0:T(8,128)(2,1)} async-done(((bf16[1,64,512]{2,1,0:T(8,128)(2,1)}), bf16[1,2048,512]{2,1,0:T(8,128)(2,1)}) %all-gather.11.cloned.1.call-update) | async-done | bytes 2097168 | tf_op jit(solution)/shard_map/all_gather | solution.py:90
  164.5 1.9 select_bitcast_fusion
  172.6 6.8 constant_dynamic-slice_fusion.4
  179.4 66.0 %all-reduce.14.cloned.1.call-done = (bf16[512,512]{1,0:T(8,128)(2,1)}, bf16[512,512]{1,0:T(8,128)(2,1)}, bf16[512,512]{1,0:T(8,128)(2,1)}) async-done(((bf16[512,512]{1,0:T(8,128)(2,1)}, bf16[512,512]{1,0:T(8,128)(2,1)}, bf16[512,512]{1,0:T(8,128)(2,1)}), (bf16[512,512]{1,0:T(8,128)(2,1)}, bf16[512,512]{1,0:T(8,128)(2,1)}, bf16[512,512]{1,0:T(8,128)(2,1)})) %all-reduce.14.cloned.1.call-update) | async-done | bytes 1572880 | tf_op jit(solution)/shard_map/psum | solution.py:19
  245.4 6.5 fusion.4
  252.2 6.5 fusion
  258.8 5.5 fusion.8
  274.9 70.0 %reduce-scatter.6.cloned.1.call-done = f32[96,512]{1,0:T(8,128)} async-done(((f32[3072,512]{1,0:T(8,128)}), f32[96,512]{1,0:T(8,128)}) %reduce-scatter.6.cloned.1.call-update) | async-done | bytes 196624 | tf_op jit(solution)/shard_map/reduce_scatter | solution.py:115
  345.0 97.1 %reduce-scatter.4.cloned.1.call-done = f32[96,512]{1,0:T(8,128)} async-done(((f32[3072,512]{1,0:T(8,128)}), f32[96,512]{1,0:T(8,128)}) %reduce-scatter.4.cloned.1.call-update) | async-done | bytes 196624 | tf_op jit(solution)/shard_map/reduce_scatter | solution.py:115
  443.5 1.7 fusion.69
  445.2 94.2 %reduce-scatter.8.cloned.1.call-done = f32[96,512]{1,0:T(8,128)} async-done(((f32[3072,512]{1,0:T(8,128)}), f32[96,512]{1,0:T(8,128)}) %reduce-scatter.8.cloned.1.call-update) | async-done | bytes 196624 | tf_op jit(solution)/shard_map/reduce_scatter | solution.py:115
  540.7 1.8 fusion.67
  542.5 1.8 fusion.64
  551.6 1.7 fusion.41
  553.6 113.2 %all-reduce.10.cloned.1.call-done = (f32[512,512]{1,0:T(8,128)}, f32[512,512]{1,0:T(8,128)}, f32[512,512]{1,0:T(8,128)}, f32[512,512]{1,0:T(8,128)}) async-done(((f32[512,512]{1,0:T(8,128)}, f32[512,512]{1,0:T(8,128)}, f32[512,512]{1,0:T(8,128)}, f32[512,512]{1,0:T(8,128)}), (f32[512,512]{1,0:T(8,128)}, f32[512,512]{1,0:T(8,128)}, f32[512,512]{1,0:T(8,128)}, ...) | async-done | bytes 4194320 | tf_op jit(solution)/shard_map/psum | solution.py:13
  667.6 264.1 %all-reduce.8.cloned.1.call-done = f32[512,512]{1,0:T(8,128)} async-done(((f32[512,512]{1,0:T(8,128)}), f32[512,512]{1,0:T(8,128)}) %all-reduce.8.cloned.1.call-update) | async-done | bytes 1048592 | tf_op jit(solution)/shard_map/psum | solution.py:81
  931.7 1.8 fusion.29
  933.6 108.5 %all-reduce.12.cloned.1.call-done = (f32[512,512]{1,0:T(8,128)}, f32[512,512]{1,0:T(8,128)}, f32[512,512]{1,0:T(8,128)}, f32[512,512]{1,0:T(8,128)}) async-done(((f32[512,512]{1,0:T(8,128)}, f32[512,512]{1,0:T(8,128)}, f32[512,512]{1,0:T(8,128)}, f32[512,512]{1,0:T(8,128)}), (f32[512,512]{1,0:T(8,128)}, f32[512,512]{1,0:T(8,128)}, f32[512,512]{1,0:T(8,128)}, ...) | async-done | bytes 4194320 | tf_op jit(solution)/shard_map/psum | solution.py:13
  1042.1 2.7 fusion.13
  1049.8 2.0 pad_maximum_fusion
  (67 shorter events, 21.1 us)
Async XLA Ops:
  7.2 159.4 %copy-start.7 = (s32[3,64]{1,0:T(4,128)S(1)}, s32[3,64]{1,0:T(4,128)}, u32[]{:S(2)}) copy-start(s32[3,64]{1,0:T(4,128)} %param.7) | copy-start | bytes 2308
  7.2 55.1 %all-gather.9.cloned.1.call-start = ((), (), s32[]{:S(2)}) async-start(), calls=%async_computation.8 | async-start | bytes 2162688 | tf_op jit(solution)/shard_map/all_gather | solution.py:90
  8.8 104.6 %all-gather.7.cloned.1.call-start = ((), (), s32[]{:S(2)}) async-start(), calls=%async_computation.7 | async-start | bytes 2162688 | tf_op jit(solution)/shard_map/all_gather | solution.py:90
  9.6 154.9 %all-gather.11.cloned.1.call-start = ((), (), s32[]{:S(2)}) async-start(), calls=%async_computation.9 | async-start | bytes 2162688 | tf_op jit(solution)/shard_map/all_gather | solution.py:90
  10.3 235.1 %all-reduce.14.cloned.1.call-start = ((), (), s32[]{:S(2)}) async-start(), calls=%async_computation.12 | async-start | bytes 3145728 | tf_op jit(solution)/shard_map/psum | solution.py:19
  166.5 178.5 %reduce-scatter.6.cloned.1.call-start = ((), (), s32[]{:S(2)}) async-start(), calls=%async_computation.4 | async-start | bytes 6488064 | tf_op jit(solution)/shard_map/reduce_scatter | solution.py:115
  252.0 190.1 %reduce-scatter.4.cloned.1.call-start = ((), (), s32[]{:S(2)}) async-start(), calls=%async_computation.3 | async-start | bytes 6488064 | tf_op jit(solution)/shard_map/reduce_scatter | solution.py:115
  258.7 280.7 %reduce-scatter.8.cloned.1.call-start = ((), (), s32[]{:S(2)}) async-start(), calls=%async_computation.5 | async-start | bytes 6488064 | tf_op jit(solution)/shard_map/reduce_scatter | solution.py:115
  264.3 177.8 %copy-start = (bf16[2,512,512]{2,1,0:T(8,128)(2,1)S(1)}, bf16[2,512,512]{2,1,0:T(8,128)(2,1)}, u32[]{:S(2)}) copy-start(bf16[2,512,512]{2,1,0:T(8,128)(2,1)} %param.8) | copy-start | bytes 3145732
  264.4 402.4 %all-reduce.10.cloned.1.call-start = ((), (), s32[]{:S(2)}) async-start(), calls=%async_computation.10 | async-start | bytes 8388608 | tf_op jit(solution)/shard_map/psum | solution.py:13
  443.5 100.7 %copy-start.3 = (f32[96,512]{1,0:T(8,128)S(1)}, f32[96,512]{1,0:T(8,128)}, u32[]{:S(2)}) copy-start(f32[96,512]{1,0:T(8,128)} %reduce-scatter.4.cloned.1.call-done) | copy-start | bytes 589828
  545.9 385.8 %all-reduce.8.cloned.1.call-start = ((), (), s32[]{:S(2)}) async-start(), calls=%async_computation.6 | async-start | bytes 2097152 | tf_op jit(solution)/shard_map/psum | solution.py:81
  553.3 488.7 %all-reduce.12.cloned.1.call-start = ((), (), s32[]{:S(2)}) async-start(), calls=%async_computation.11 | async-start | bytes 8388608 | tf_op jit(solution)/shard_map/psum | solution.py:13
  931.7 110.4 %copy-start.2 = (f32[512,512]{1,0:T(8,128)S(1)}, f32[512,512]{1,0:T(8,128)}, u32[]{:S(2)}) copy-start(f32[512,512]{1,0:T(8,128)} %all-reduce.8.cloned.1.call-done) | copy-start | bytes 3145732
  1042.1 2.7 copy-start.1
  1042.1 2.8 copy-start.6
  1044.8 1.2 copy-start.4
  1044.9 2.2 copy-start.5
Sparse Core Ops, SparseCore 0:
  11.1 51.0 all-gather.8
  65.4 47.9 all-gather.6
  116.5 47.9 all-gather.10
  167.0 78.4 all-reduce.13
  252.1 92.8 reduce-scatter.5
  348.9 93.1 reduce-scatter.3
  446.1 93.2 reduce-scatter.7
  546.1 120.6 all-reduce.9
  672.2 259.4 all-reduce.7
  934.2 107.8 all-reduce.11
